TPU v7x, 1024 devices: a whole 4x8x16 slice. The times are simulated.
1024 devices in a mesh: dp: 128 (over z, x, core), tensor: 8 (over y).
Axes of the slice: x: 4, y: 8, z: 16, core: 2. Of those that a mesh axis runs over, the one named last changes fastest.
Arguments:
- activations: bfloat16 [24576, 8192], P('dp'), may hold values from -6 to 6
- out_grads: bfloat16 [24576, 2048], P('dp', 'tensor'), may hold values from -6 to 6
- kv_weight: bfloat16 [8192, 2048], P('dp', 'tensor'), may hold values from -0.125 to 0.125
- block_ids: int32 [8, 6], P('tensor'), may hold values from 0 to 127, as said below
- block_owner: int32 [8, 6], P('tensor'), may hold values from 0 to 127, as said below
Outputs:
- input_grad: bfloat16 [24576, 8192], P('dp', 'tensor')
- owned_grads: float32 [8, 256, 128, 128], P('tensor', 'dp')
Inputs may be any that keep to these rules, and one draw needn't show every extreme that they name: `block_ids`: within one shard the 6 block numbers are distinct. `block_owner`: within one shard no owner holds more than 2 blocks, and some owner holds exactly 2.
All inputs are finite; a program needn't handle non-finite values.
Results may differ from a plain program's by a relative error of at most 0.001.
Values may be sent and summed in bfloat16 or wider, within the bound.
A program may use at most 32 MiB of HBM per device.

v0:
```python
import math

import jax
import jax.numpy as jnp
from jax import lax
from jax.sharding import PartitionSpec as P

BLK = 128
NB = 6
CAP = 2


def local(activations, out_grads, kv_weight, block_ids, block_owner):
    tokens_here = activations.shape[0]
    width = activations.shape[1]
    shard_cols = out_grads.shape[1]
    col_blocks = shard_cols // BLK
    groups_dp = lax.axis_size("dp")
    numbers = block_ids[0]
    row_index = numbers // col_blocks
    col_index = numbers % col_blocks
    x_blocks = activations.reshape(tokens_here, width // BLK, BLK)[:, row_index, :]
    g_blocks = out_grads.reshape(tokens_here, col_blocks, BLK)[:, col_index, :]
    partial_blocks = jnp.einsum(
        "tnb,tnc->nbc", x_blocks, g_blocks, preferred_element_type=jnp.float32
    )
    owners_row = block_owner[0]
    position = jnp.arange(NB, dtype=jnp.int32)
    same_owner = owners_row[:, None] == owners_row[None, :]
    before = position[None, :] < position[:, None]
    ranks = jnp.sum((same_owner & before).astype(jnp.int32), axis=1)
    slot_range = jnp.arange(CAP, dtype=jnp.int32)
    scale_factor = 1.0 / math.sqrt(groups_dp * tokens_here)
    summed_blocks = lax.psum(partial_blocks, "dp")
    my_index = lax.axis_index("dp")
    selector = ((owners_row[None, :] == my_index) & (ranks[None, :] == slot_range[:, None])).astype(
        jnp.float32
    )
    owned = (
        jnp.einsum("sj,jbc->sbc", selector, summed_blocks, precision=lax.Precision.HIGHEST)
        * scale_factor
    )
    row_terms = lax.dot_general(
        out_grads,
        lax.all_gather(kv_weight, "dp", axis=0, tiled=True),
        (((1,), (1,)), ((), ())),
        preferred_element_type=jnp.float32,
    )
    input_grad = lax.psum_scatter(row_terms, "tensor", scatter_dimension=1, tiled=True).astype(
        jnp.bfloat16
    )
    return (input_grad, owned[None])


def solution(mesh):
    return jax.shard_map(
        local,
        mesh=mesh,
        in_specs=(
            P("dp", None),
            P("dp", "tensor"),
            P("dp", "tensor"),
            P("tensor", None),
            P("tensor", None),
        ),
        out_specs=(P("dp", "tensor"), P("tensor", "dp", None, None)),
        check_vma=False,
    )
```

profile of v0, /device:TPU:1, one launch (start us, length us, event | category | flops | bytes accessed | tf_op | source)
XLA Modules:
  0.0 601.8 jit_solution(4983393612398084813)
XLA Ops:
  7.2 0.0 copy-start
  7.2 0.0 all-gather.2.cloned.1.call-start
  7.2 0.7 all-gather.2.cloned.1.call-update
  7.9 0.0 all-reduce.2.cloned.1.call-start
  8.0 0.8 fusion.11
  8.8 0.9 copy_bitcast_fusion.1
  9.7 0.6 gather_fusion.1
  10.3 0.0 copy-done
  10.3 0.0 copy-start.1
  10.3 2.5 copy_bitcast_fusion
  12.9 3.2 gather_fusion
  16.1 2.0 fusion.2
  18.1 0.0 all-reduce.2.cloned.1.call-update
  18.1 0.0 reduce-scatter.2.cloned.1.call-start
  18.2 152.3 %all-gather.2.cloned.1.call-done = bf16[8192,256]{1,0:T(8,128)(2,1)} async-done(((bf16[64,256]{1,0:T(8,128)(2,1)}), bf16[8192,256]{1,0:T(8,128)(2,1)}) %all-gather.2.cloned.1.call-update) | async-done | bytes 4194320 | tf_op jit(solution)/shard_map/all_gather | solution.py:45
  170.5 0.0 copy-done.1
  170.5 6.4 %fusion.14 = f32[192,8192]{1,0:T(8,128)} fusion(bf16[192,256]{1,0:T(8,128)(2,1)S(1)} %copy-done.1, bf16[8192,256]{1,0:T(8,128)(2,1)} %all-gather.2.cloned.1.call-done), kind=kOutput, calls=%fused_computation.32 | convolution fusion | flops 805306368 | bytes 10584064 | tf_op jit(solution)/shard_map/dot_general | solution.py:43
  176.9 0.0 copy-start.2
  176.9 0.0 reduce-scatter.2.cloned.1.call-update
  176.9 0.6 copy-done.2
  177.5 0.2 convert_reduce_fusion
  177.7 332.1 %all-reduce.2.cloned.1.call-done = f32[6,128,128]{2,1,0:T(8,128)} async-done(((f32[6,128,128]{2,1,0:T(8,128)}), f32[6,128,128]{2,1,0:T(8,128)}) %all-reduce.2.cloned.1.call-update) | async-done | bytes 393232 | tf_op jit(solution)/shard_map/psum | solution.py:34
  509.8 1.6 fusion
  511.4 0.7 copy.16
  512.0 81.3 %reduce-scatter.2.cloned.1.call-done = f32[192,1024]{1,0:T(8,128)} async-done(((f32[192,8192]{1,0:T(8,128)}), f32[192,1024]{1,0:T(8,128)}) %reduce-scatter.2.cloned.1.call-update) | async-done | bytes 786448 | tf_op jit(solution)/shard_map/reduce_scatter | solution.py:49
  593.3 1.9 convert_element_type.7
  (2 shorter events, 0.0 us)
Async XLA Ops:
  7.2 3.2 copy-start
  7.2 163.3 %all-gather.2.cloned.1.call-start = ((), (), s32[]{:S(2)}) async-start(), calls=%async_computation.1 | async-start | bytes 4227072 | tf_op jit(solution)/shard_map/all_gather | solution.py:45
  7.9 501.9 %all-reduce.2.cloned.1.call-start = ((), (), s32[]{:S(2)}) async-start(), calls=%async_computation.3 | async-start | bytes 786432 | tf_op jit(solution)/shard_map/psum | solution.py:34
  10.3 160.2 %copy-start.1 = (bf16[192,256]{1,0:T(8,128)(2,1)S(1)}, bf16[192,256]{1,0:T(8,128)(2,1)}, u32[]{:S(2)}) copy-start(bf16[192,256]{1,0:T(8,128)(2,1)} %param.6) | copy-start | bytes 294916
  18.1 575.2 %reduce-scatter.2.cloned.1.call-start = ((), (), s32[]{:S(2)}) async-start(), calls=%async_computation.2 | async-start | bytes 7077888 | tf_op jit(solution)/shard_map/reduce_scatter | solution.py:49
  176.9 0.7 copy-start.2
Sparse Core Ops, SparseCore 0:
  12.3 158.1 all-gather.1
  174.5 335.2 all-reduce.1
  513.6 79.6 reduce-scatter.1
where the time goes:
time: 602 us
  waiting for transfers between devices  566 us (94%)
  between operations  13.8 us (2%)
  matrix products  9.95 us (2%)
  local copies, waits for them, and re-layouts  8.56 us (1%)
    psum x1, waiting for transfers between devices, local(): summed_blocks = lax.psum(partial_blocks, 'dp')  332 us
    all_gather x1, waiting for transfers between devices, local(): lax.all_gather(kv_weight, 'dp', axis=0, tiled=True)  152 us
    reduce_scatter x1, waiting for transfers between devices, local(): lax.psum_scatter(row_terms, 'tensor', scatter_dimension=1, tiled=True)  81.3 us
  transfers between devices with their start and end apart: 3, of which 3 were waited for; matrix products, arithmetic and copies ran while one was open for 3% of the time, Pallas kernels for 0%

commit v1 on v0

v1 whole, which is shorter than its diff:
```python
import jax
import jax.numpy as jnp
from jax import lax
from jax.experimental import pallas as pl
from jax.experimental.pallas import tpu as pltpu
from jax.sharding import PartitionSpec as P

MESH = pl.DeviceIdType.MESH
NX, NY, NZ = 4, 8, 16
BLK = 128
NB = 6
CAP = 2
PIECES = 12
SCALE = 24576.0 ** -0.5


def block_terms(ids_ref, owner_ref, x_hbm, g_hbm, part_ref, sel_ref, xbuf, gbuf, sems):
    dp = lax.axis_index("dp")
    c, x, z = dp % 2, (dp // 2) % NX, dp // 8
    copies = [pltpu.make_async_copy(g_hbm, gbuf, sems.at[NB])]
    for n in range(NB):
        rows = pl.multiple_of((ids_ref[0, n] // 2) * BLK, BLK)
        copies.append(pltpu.make_async_copy(x_hbm.at[:, pl.ds(rows, BLK)], xbuf.at[n], sems.at[n]))
    for copy in copies:
        copy.start()
    owners = [owner_ref[0, n] for n in range(NB)]
    ranks = []
    for n in range(NB):
        r = jnp.int32(0)
        for m in range(n):
            r = r + (owners[m] == owners[n]).astype(jnp.int32)
        ranks.append(r)
    for i in range(8):
        to = (z * NX + (x + i // 2) % NX) * 2 + (c + i % 2) % 2
        for s in range(CAP):
            for n in range(NB):
                hit = (owners[n] == to) & (ranks[n] == s)
                sel_ref[0, (i * CAP + s) * NB + n] = jnp.where(hit, jnp.float32(1), jnp.float32(0))
    copies[0].wait()
    for n in range(NB):
        copies[n + 1].wait()
        gb = gbuf[:, pl.ds(pl.multiple_of((ids_ref[0, n] % 2) * BLK, BLK), BLK)]
        term = lax.dot_general(
            xbuf[n], gb, (((0,), (0,)), ((), ())), preferred_element_type=jnp.float32
        )
        part_ref[0, n] = term[:64]
        part_ref[1, n] = term[64:]


def kernel(
    sel_ref, part_hbm, g_hbm, w_hbm, out_ref, owned_ref,
    wbuf, wown, gbuf, acc, part, half, xsum, xrecv, zsum, zrecv, mine, full, pick, got,
    load_sem, shard_ss, zs, xs, rs, cs, gs, as_, zr, xr, xl, x2, cr, gr, ar,
):
    dp = lax.axis_index("dp")
    y = lax.axis_index("tensor")
    c = dp % 2
    x = (dp // 2) % NX
    z = dp // 8
    role = (z - 2 * y + NZ) % NZ
    hown = role % 2
    slab = role < 2
    xp, xm, xo = (x + 1) % NX, (x + 3) % NX, (x + 2) % NX

    def dev(xx, yy, zz, cc):
        return ((zz * NX + xx) * 2 + cc, yy)

    def col(xx, hh, cc):
        return pl.multiple_of(hh * 512 + xx * 128 + cc * 64, 64)

    def unit(j, xx, hh, cc):
        return wbuf.at[j, pl.ds(col(xx, hh, cc), 64), :]

    def send(src, dst, ssem, rsem, to):
        pltpu.make_async_remote_copy(
            src_ref=src, dst_ref=dst, send_sem=ssem, recv_sem=rsem, device_id=to, device_id_type=MESH
        ).start()

    def desc(ref, ssem, rsem):
        return pltpu.make_async_remote_copy(
            src_ref=ref, dst_ref=ref, send_sem=ssem, recv_sem=rsem,
            device_id=dev(x, y, z, 1 - c), device_id_type=MESH,
        )

    def wait_recv(ref, rsem):
        desc(ref, cs, rsem).wait_recv()

    def wait_send(ref, ssem):
        desc(ref, ssem, gr).wait_send()

    load_p = pltpu.make_async_copy(part_hbm.at[c], part, load_sem.at[0])
    load_g = pltpu.make_async_copy(g_hbm, gbuf.at[y], load_sem.at[1])
    load_w = pltpu.make_async_copy(w_hbm, wown, load_sem.at[2])
    load_w.start()
    load_g.start()
    load_p.start()
    local_w = pltpu.make_async_copy(w_hbm, unit(0, x, hown, c), load_sem.at[3])

    @pl.when(slab)
    def _():
        local_w.start()

    barrier = pltpu.get_barrier_semaphore()
    peers = [dev(x, (y + i) % NY, z, c) for i in range(1, NY)]
    peers += [dev(x, y, (z + i) % NZ, c) for i in range(1, NZ)]
    peers += [dev((x + i) % NX, y, z, c) for i in range(1, NX)]
    peers += [dev((x + i) % NX, y, z, 1 - c) for i in range(NX)]
    for p in peers:
        pl.semaphore_signal(barrier, inc=1, device_id=p, device_id_type=MESH)

    load_g.wait()
    load_p.wait()
    load_w.wait()
    pl.semaphore_wait(barrier, len(peers))

    yd = z // 2
    d = (y - yd + NY) % NY
    jd = jnp.where(d == 0, 0, jnp.where(d <= 4, 2 * d - 1, 16 - 2 * d))

    @pl.when(jnp.logical_not(slab))
    def _():
        send(wown, unit(jd, x, hown, c), shard_ss, zr.at[2 * jd + z % 2], dev(x, yd, z, c))

    send(part_hbm.at[1 - c], half, as_.at[0], ar.at[0], dev(x, y, z, 1 - c))

    def spread(j, h, order):
        u = unit(j, x, h, c)
        k = 2 * j + h
        source = slab & (h == hown)
        up = jnp.where(
            role == 0, 1, jnp.where(role == 1, 4, 1)
        )
        down = jnp.where(role == 0, -4, jnp.where(role == 1, -1, -1))
        go_up = source | ((role >= 5) & (role <= 7)) | ((role >= 12) & (role <= 14))
        go_down = source | ((role >= 3) & (role <= 5)) | ((role >= 10) & (role <= 12))

        @pl.when(go_up)
        def _():
            send(u, u, zs, zr.at[k], dev(x, y, (z + up + NZ) % NZ, c))

        @pl.when(go_down)
        def _():
            send(u, u, zs, zr.at[k], dev(x, y, (z + down + NZ) % NZ, c))

        @pl.when(source)
        def _():
            far = jnp.where(role == 0, 5, -5)
            send(u, u, zs, zr.at[k], dev(x, y, (z + far + NZ) % NZ, c))

        send(u, u, xs, xr.at[j], dev(xp, y, z, c))
        send(u, u, xs, xl.at[j], dev(xm, y, z, c))
        send(u, u, cs, cr.at[j], dev(x, y, z, 1 - c))

    def take(j, h):
        wait_recv(unit(j, x, h, c), zr.at[2 * j + h])
        spread(j, h, 0)

    def core_step():
        wait_recv(half, ar.at[0])
        s = part[...] + half[...]
        for i in range(NX):
            xsum[i] = s[:, 16 * i:16 * (i + 1), :]
        for i in range(1, NX):
            xx = (x + i) % NX
            send(xsum.at[xx], xrecv.at[x], as_.at[1], ar.at[1], dev(xx, y, z, c))
        xrecv[x] = xsum[x]

    def x_step():
        wait_recv(xrecv.at[pl.ds(0, 3)], ar.at[1])
        s = xrecv[0] + xrecv[1] + xrecv[2] + xrecv[3]
        zsum[...] = s.reshape(PIECES, 8, 128)

        def body(i, carry):
            @pl.when(i != z)
            def _():
                send(zsum.at[i], zrecv.at[z], as_.at[2], ar.at[2], dev(x, y, i, c))

            return carry

        lax.fori_loop(0, PIECES, body, 0)

    def z_step():
        @pl.when(z < PIECES)
        def _():
            zrecv[z] = zsum[jnp.minimum(z, PIECES - 1)]
            wait_recv(zrecv.at[pl.ds(0, NZ - 1)], ar.at[2])
            s = zrecv[0]
            for i in range(1, NZ):
                s = s + zrecv[i]
            mine[...] = s * SCALE
            full[jnp.minimum(z, PIECES - 1)] = s * SCALE

            def body(i, carry):
                zz = (z + i) % NZ
                send(mine, full.at[jnp.minimum(z, PIECES - 1)], as_.at[3], ar.at[3], dev(x, y, zz, c))
                return carry

            lax.fori_loop(1, NZ, body, 0)

    def send_g():
        for i in (1, 7, 2, 6, 3, 5, 4):
            send(gbuf.at[y], gbuf.at[y], gs, gr, dev(x, (y + i) % NY, z, c))

    @pl.when(slab)
    def _():
        local_w.wait()
        spread(0, hown, 0)
        core_step()
        take(1, hown)
        take(2, hown)
        x_step()
        send_g()

        def body(j, carry):
            take(j, hown)
            return carry

        lax.fori_loop(3, 8, body, 0)

        def body2(j, carry):
            take(j, 1 - hown)
            return carry

        lax.fori_loop(0, 8, body2, 0)
        z_step()

    dist = jnp.where(role >= 9, jnp.abs(role - 12), jnp.abs(role - 5))
    jz = jnp.where(dist == 0, 5, jnp.where(dist == 1, 4, jnp.where(dist == 2, 2, 1)))

    @pl.when(jnp.logical_not(slab))
    def _():
        core_step()
        x_step()
        send_g()

        def body(j, carry):
            @pl.when(j == jz)
            def _():
                z_step()

            take(j, 0)
            take(j, 1)
            return carry

        lax.fori_loop(0, 8, body, 0)

    def body(j, carry):
        wait_recv(wbuf.at[j, pl.ds(0, 128), :], xr.at[j])
        even = j % 2 == 0
        for h in range(2):
            u = unit(j, xm, h, c)

            @pl.when(even)
            def _():
                send(u, u, rs, x2.at[j], dev(xp, y, z, c))

            send(u, u, cs, cr.at[j], dev(x, y, z, 1 - c))
        wait_recv(wbuf.at[j, pl.ds(0, 128), :], xl.at[j])
        for h in range(2):
            u = unit(j, xp, h, c)

            @pl.when(jnp.logical_not(even))
            def _():
                send(u, u, rs, x2.at[j], dev(xm, y, z, c))

            send(u, u, cs, cr.at[j], dev(x, y, z, 1 - c))
        return carry

    lax.fori_loop(0, 8, body, 0)

    @pl.when(z < PIECES)
    def _():
        wait_recv(full.at[pl.ds(0, PIECES - 1)], ar.at[3])

    @pl.when(z >= PIECES)
    def _():
        wait_recv(full, ar.at[3])

    row0 = pl.multiple_of(c * 64 + x * 16, 16)
    for i in range(8):
        xx, cc = (x + i // 2) % NX, (c + i % 2) % 2
        to = (z * NX + xx) * 2 + cc
        for s in range(CAP):
            total = jnp.zeros((2, 8, 128), jnp.float32)
            for n in range(NB):
                total = total + full[pl.ds(2 * n, 2)] * sel_ref[0, (i * CAP + s) * NB + n]
            if i == 0:
                got[s, pl.ds(row0, 16), :] = total.reshape(16, 128)
            else:
                pick[i - 1, s] = total.reshape(16, 128)
        if i > 0:
            send(pick.at[i - 1], got.at[:, pl.ds(row0, 16), :], as_.at[4], ar.at[4], (to, y))

    wait_recv(gbuf.at[pl.ds(0, 7)], gr)

    def product(j):
        shift = ((j + 1) // 2) * (2 * (j % 2) - 1)
        yw = (y + shift + NY) % NY
        wait_recv(wbuf.at[j, pl.ds(0, 512), :], cr.at[j])
        return lax.dot_general(
            gbuf[yw], wbuf[j], (((1,), (1,)), ((), ())), preferred_element_type=jnp.float32
        )

    def fetch(j):
        wait_recv(wbuf.at[j, pl.ds(0, 128), :], x2.at[j])
        for h in range(2):
            u = unit(j, xo, h, c)
            send(u, u, cs, cr.at[j], dev(x, y, z, 1 - c))

    acc[...] = jnp.zeros_like(acc)
    fetch(0)

    def body(j, carry):
        fetch(j)
        acc[...] += product(j - 1)
        return carry

    lax.fori_loop(1, 8, body, 0)
    out_ref[...] = (acc[...] + product(7)).astype(jnp.bfloat16)

    wait_recv(got.at[:, pl.ds(0, 112), :], ar.at[4])
    owned_ref[0] = got[...]

    @pl.when(jnp.logical_not(slab))
    def _():
        wait_send(wown, shard_ss)

    @pl.when(slab)
    def _():
        wait_send(wbuf.at[pl.ds(0, 3), pl.ds(0, 512), :], zs)

    @pl.when((role == 5) | (role == 12))
    def _():
        wait_send(wbuf.at[pl.ds(0, 2)], zs)

    @pl.when(
        (role == 3) | (role == 4) | (role == 6) | (role == 7)
        | (role == 10) | (role == 11) | (role == 13) | (role == 14)
    )
    def _():
        wait_send(wbuf.at[pl.ds(0, 1)], zs)

    wait_send(wbuf.at[pl.ds(0, 2)], xs)
    wait_send(wbuf.at[pl.ds(0, 1)], rs)
    wait_send(wbuf.at[pl.ds(0, 4)], cs)
    wait_send(gbuf.at[pl.ds(0, 7)], gs)
    wait_send(half, as_.at[0])
    wait_send(xsum.at[pl.ds(0, 3)], as_.at[1])

    @pl.when(z < PIECES)
    def _():
        wait_send(zsum.at[pl.ds(0, PIECES - 1)], as_.at[2])
        wait_send(zrecv.at[pl.ds(0, NZ - 1)], as_.at[3])

    @pl.when(z >= PIECES)
    def _():
        wait_send(zsum, as_.at[2])

    wait_send(pick, as_.at[4])


def local(activations, out_grads, kv_weight, block_ids, block_owner):
    f32, bf16 = jnp.float32, jnp.bfloat16
    dma = pltpu.SemaphoreType.DMA
    any_space = pl.BlockSpec(memory_space=pl.ANY)
    smem = pl.BlockSpec(memory_space=pltpu.SMEM)
    vmem = pl.BlockSpec(memory_space=pltpu.VMEM)
    part, sel = pl.pallas_call(
        block_terms,
        name="block_terms",
        out_shape=(
            jax.ShapeDtypeStruct((2, NB, 64, BLK), f32),
            jax.ShapeDtypeStruct((1, 8 * CAP * NB), f32),
        ),
        in_specs=[smem] * 2 + [any_space] * 2,
        out_specs=(vmem, smem),
        scratch_shapes=[
            pltpu.VMEM((NB, 192, BLK), bf16),
            pltpu.VMEM((192, 256), bf16),
            dma((NB + 1,)),
        ],
    )(block_ids, block_owner, activations, out_grads)
    return pl.pallas_call(
        kernel,
        name="kv_backward",
        out_shape=(
            jax.ShapeDtypeStruct((192, 1024), bf16),
            jax.ShapeDtypeStruct((1, CAP, BLK, BLK), f32),
        ),
        in_specs=[smem] + [any_space] * 3,
        out_specs=(vmem, vmem),
        scratch_shapes=[
            pltpu.VMEM((8, 1024, 256), bf16),
            pltpu.VMEM((64, 256), bf16),
            pltpu.VMEM((8, 192, 256), bf16),
            pltpu.VMEM((192, 1024), f32),
            pltpu.VMEM((NB, 64, BLK), f32),
            pltpu.VMEM((NB, 64, BLK), f32),
            pltpu.VMEM((NX, NB, 16, BLK), f32),
            pltpu.VMEM((NX, NB, 16, BLK), f32),
            pltpu.VMEM((PIECES, 8, BLK), f32),
            pltpu.VMEM((NZ, 8, BLK), f32),
            pltpu.VMEM((8, BLK), f32),
            pltpu.VMEM((PIECES, 8, BLK), f32),
            pltpu.VMEM((7, CAP, 16, BLK), f32),
            pltpu.VMEM((CAP, BLK, BLK), f32),
            dma((4,)), dma, dma, dma, dma, dma, dma, dma((5,)),
            dma((16,)), dma((8,)), dma((8,)), dma((8,)), dma((8,)), dma, dma((5,)),
        ],
        compiler_params=pltpu.CompilerParams(collective_id=0, has_side_effects=True),
    )(sel, part, out_grads, kv_weight)


def solution(mesh):
    return jax.shard_map(
        local,
        mesh=mesh,
        in_specs=(
            P("dp", None),
            P("dp", "tensor"),
            P("dp", "tensor"),
            P("tensor", None),
            P("tensor", None),
        ),
        out_specs=(P("dp", "tensor"), P("tensor", "dp", None, None)),
        check_vma=False,
    )
```

time: 602 us -> 75.6 us (0.13)
  the two profiles are of different devices: /device:TPU:1 before, /device:TPU:57 now
where the time goes in v1:
time: 75.6 us; the launch traced here: 75.3 us
  Pallas kernels  71.3 us (94%)
  local copies, waits for them, and re-layouts  3.33 us (4%)
    pallas_call x1, Pallas kernels, local(): pl.pallas_call(kernel, name='kv_backward', out_shape=(jax.ShapeDtypeStruc...  67.7 us
    pallas_call x1, Pallas kernels, local(): pl.pallas_call(block_terms, name='block_terms', out_shape=(jax.ShapeDtype...  3.6 us
    unnamed x2, local copies, waits for them, and re-layouts  3.33 us

profile of v1, /device:TPU:57, one launch (start us, length us, event | category | flops | bytes accessed | tf_op | source)
XLA Modules:
  0.0 75.3 jit_solution(1907182793339799079)
XLA Ops:
  0.6 3.6 %block_terms.1 = (f32[2,6,64,128]{3,2,1,0:T(8,128)}, f32[1,96]{1,0:T(1,128)}) custom-call(s32[1,6]{1,0:T(1,128)} %ids_ref.1, s32[1,6]{1,0:T(1,128)} %owner_ref.1, bf16[192,8192]{1,0:T(8,128)(2,1)} %x_hbm.1, bf16[192,256]{1,0:T(8,128)(2,1)} %g_hbm.3), custom_call_target="tpu_custom_call" | custom-call | tf_op jit(solution)/shard_map/block_terms/pallas_call | solution.py:368
  4.2 67.7 %kv_backward.1 = (bf16[192,1024]{1,0:T(8,128)(2,1)}, f32[1,2,128,128]{3,2,1,0:T(8,128)}) custom-call(f32[1,96]{1,0:T(1,128)} %get-tuple-element.4.sel_ref, f32[2,6,64,128]{3,2,1,0:T(8,128)} %get-tuple-element.5.part_hbm, bf16[192,256]{1,0:T(8,128)(2,1)} %g_hbm.3, bf16[64,256]{1,0:T(8,128)(2,1)} %w_hbm.1), custom_call_target="tpu_custom_call" | custom-call | tf_op jit(solution)/shard_map/kv_backward/pallas_call | solution.py:383
  72.0 1.8 %copy.9 = bf16[192,1024]{1,0:T(8,128)(2,1)} copy(bf16[192,1024]{1,0:T(8,128)(2,1)} %get-tuple-element.8) | data formatting | bytes 786432
  73.7 1.6 %copy.10 = f32[1,2,128,128]{3,2,1,0:T(8,128)} copy(f32[1,2,128,128]{3,2,1,0:T(8,128)} %get-tuple-element.9) | data formatting | bytes 262144

commit v2 on v1

--- a/solution.py
+++ b/solution.py
@@ -10,7 +10,7 @@
 BLK = 128
 NB = 6
 CAP = 2
-PIECES = 12
+PIECES = 6
 SCALE = 24576.0 ** -0.5
 
 
@@ -60,6 +60,10 @@
     role = (z - 2 * y + NZ) % NZ
     hown = role % 2
     slab = role < 2
+    piece = (role + 2) % NZ
+    owner = piece < PIECES
+    spot = jnp.minimum(piece, PIECES - 1)
+    stop = (role == 3) | (role == 5) | (role == 7) | (role == 10) | (role == 12) | (role == 14)
     xp, xm, xo = (x + 1) % NX, (x + 3) % NX, (x + 2) % NX
 
     def dev(xx, yy, zz, cc):
@@ -123,29 +127,23 @@
 
     send(part_hbm.at[1 - c], half, as_.at[0], ar.at[0], dev(x, y, z, 1 - c))
 
-    def spread(j, h, order):
+    def spread(j, h):
         u = unit(j, x, h, c)
         k = 2 * j + h
         source = slab & (h == hown)
-        up = jnp.where(
-            role == 0, 1, jnp.where(role == 1, 4, 1)
-        )
-        down = jnp.where(role == 0, -4, jnp.where(role == 1, -1, -1))
-        go_up = source | ((role >= 5) & (role <= 7)) | ((role >= 12) & (role <= 14))
-        go_down = source | ((role >= 3) & (role <= 5)) | ((role >= 10) & (role <= 12))
-
-        @pl.when(go_up)
+        up = jnp.where(role == 0, 3, jnp.where(role == 1, 2, jnp.where((role == 3) | (role == 5), 2, 1)))
+        down = jnp.where(role == 0, 2, jnp.where(role == 1, 3, jnp.where((role == 12) | (role == 14), 2, 1)))
+        go = source | stop
+
+        @pl.when(go)
         def _():
-            send(u, u, zs, zr.at[k], dev(x, y, (z + up + NZ) % NZ, c))
-
-        @pl.when(go_down)
-        def _():
-            send(u, u, zs, zr.at[k], dev(x, y, (z + down + NZ) % NZ, c))
+            send(u, u, zs, zr.at[k], dev(x, y, (z + up) % NZ, c))
+            send(u, u, zs, zr.at[k], dev(x, y, (z - down + NZ) % NZ, c))
 
         @pl.when(source)
         def _():
-            far = jnp.where(role == 0, 5, -5)
-            send(u, u, zs, zr.at[k], dev(x, y, (z + far + NZ) % NZ, c))
+            other = jnp.where(role == 0, 1, NZ - 1)
+            send(u, u, zs, zr.at[k], dev(x, y, (z + other) % NZ, c))
 
         send(u, u, xs, xr.at[j], dev(xp, y, z, c))
         send(u, u, xs, xl.at[j], dev(xm, y, z, c))
@@ -153,7 +151,7 @@
 
     def take(j, h):
         wait_recv(unit(j, x, h, c), zr.at[2 * j + h])
-        spread(j, h, 0)
+        spread(j, h)
 
     def core_step():
         wait_recv(half, ar.at[0])
@@ -168,34 +166,33 @@
     def x_step():
         wait_recv(xrecv.at[pl.ds(0, 3)], ar.at[1])
         s = xrecv[0] + xrecv[1] + xrecv[2] + xrecv[3]
-        zsum[...] = s.reshape(PIECES, 8, 128)
+        zsum[...] = s
 
         def body(i, carry):
-            @pl.when(i != z)
+            @pl.when(i != piece)
             def _():
-                send(zsum.at[i], zrecv.at[z], as_.at[2], ar.at[2], dev(x, y, i, c))
+                to = (i + 14 + 2 * y) % NZ
+                send(zsum.at[i], zrecv.at[z], as_.at[2], ar.at[2], dev(x, y, to, c))
 
             return carry
 
         lax.fori_loop(0, PIECES, body, 0)
 
     def z_step():
-        @pl.when(z < PIECES)
-        def _():
-            zrecv[z] = zsum[jnp.minimum(z, PIECES - 1)]
-            wait_recv(zrecv.at[pl.ds(0, NZ - 1)], ar.at[2])
-            s = zrecv[0]
-            for i in range(1, NZ):
-                s = s + zrecv[i]
-            mine[...] = s * SCALE
-            full[jnp.minimum(z, PIECES - 1)] = s * SCALE
-
-            def body(i, carry):
-                zz = (z + i) % NZ
-                send(mine, full.at[jnp.minimum(z, PIECES - 1)], as_.at[3], ar.at[3], dev(x, y, zz, c))
-                return carry
-
-            lax.fori_loop(1, NZ, body, 0)
+        zrecv[z] = zsum[spot]
+        wait_recv(zrecv.at[pl.ds(0, NZ - 1)], ar.at[2])
+        s = zrecv[0]
+        for i in range(1, NZ):
+            s = s + zrecv[i]
+        mine[...] = s * SCALE
+        full[spot] = s * SCALE
+
+        def body(i, carry):
+            zz = (z + i) % NZ
+            send(mine, full.at[spot], as_.at[3], ar.at[3], dev(x, y, zz, c))
+            return carry
+
+        lax.fori_loop(1, NZ, body, 0)
 
     def send_g():
         for i in (1, 7, 2, 6, 3, 5, 4):
@@ -204,45 +201,60 @@
     @pl.when(slab)
     def _():
         local_w.wait()
-        spread(0, hown, 0)
-        core_step()
-        take(1, hown)
-        take(2, hown)
-        x_step()
-        send_g()
+        spread(0, hown)
 
         def body(j, carry):
             take(j, hown)
             return carry
 
-        lax.fori_loop(3, 8, body, 0)
+        lax.fori_loop(1, 8, body, 0)
+        core_step()
+        take(0, 1 - hown)
+        take(1, 1 - hown)
+        x_step()
+        send_g()
 
         def body2(j, carry):
             take(j, 1 - hown)
             return carry
 
-        lax.fori_loop(0, 8, body2, 0)
+        lax.fori_loop(2, 8, body2, 0)
         z_step()
 
-    dist = jnp.where(role >= 9, jnp.abs(role - 12), jnp.abs(role - 5))
-    jz = jnp.where(dist == 0, 5, jnp.where(dist == 1, 4, jnp.where(dist == 2, 2, 1)))
-
-    @pl.when(jnp.logical_not(slab))
+    def units(start, stop_at):
+        def body(j, carry):
+            take(j, 0)
+            take(j, 1)
+            return carry
+
+        lax.fori_loop(start, stop_at, body, 0)
+
+    first = (role == 3) | (role == 14)
+
+    @pl.when(first)
+    def _():
+        units(0, 3)
+        core_step()
+        units(3, 5)
+        x_step()
+        send_g()
+        units(5, 8)
+        z_step()
+
+    side = (role == 2) | (role == 15)
+
+    @pl.when(jnp.logical_not(slab | first))
     def _():
         core_step()
         x_step()
         send_g()
-
-        def body(j, carry):
-            @pl.when(j == jz)
-            def _():
-                z_step()
-
-            take(j, 0)
-            take(j, 1)
-            return carry
-
-        lax.fori_loop(0, 8, body, 0)
+        units(0, 6)
+
+        @pl.when(side)
+        def _():
+            z_step()
+
+        units(6, 8)
 
     def body(j, carry):
         wait_recv(wbuf.at[j, pl.ds(0, 128), :], xr.at[j])
@@ -268,28 +280,35 @@
 
     lax.fori_loop(0, 8, body, 0)
 
-    @pl.when(z < PIECES)
-    def _():
-        wait_recv(full.at[pl.ds(0, PIECES - 1)], ar.at[3])
-
-    @pl.when(z >= PIECES)
-    def _():
-        wait_recv(full, ar.at[3])
-
-    row0 = pl.multiple_of(c * 64 + x * 16, 16)
-    for i in range(8):
-        xx, cc = (x + i // 2) % NX, (c + i % 2) % 2
-        to = (z * NX + xx) * 2 + cc
-        for s in range(CAP):
-            total = jnp.zeros((2, 8, 128), jnp.float32)
-            for n in range(NB):
-                total = total + full[pl.ds(2 * n, 2)] * sel_ref[0, (i * CAP + s) * NB + n]
-            if i == 0:
-                got[s, pl.ds(row0, 16), :] = total.reshape(16, 128)
-            else:
-                pick[i - 1, s] = total.reshape(16, 128)
-        if i > 0:
-            send(pick.at[i - 1], got.at[:, pl.ds(row0, 16), :], as_.at[4], ar.at[4], (to, y))
+    def deliver():
+        @pl.when(owner)
+        def _():
+            wait_recv(full.at[pl.ds(0, PIECES - 1)], ar.at[3])
+
+        @pl.when(jnp.logical_not(owner))
+        def _():
+            wait_recv(full, ar.at[3])
+
+        row0 = pl.multiple_of(c * 64 + x * 16, 16)
+        for i in range(8):
+            xx, cc = (x + i // 2) % NX, (c + i % 2) % 2
+            to = (z * NX + xx) * 2 + cc
+            for s in range(CAP):
+                total = jnp.zeros((16, 128), jnp.float32)
+                for n in range(NB):
+                    total = total + full[n] * sel_ref[0, (i * CAP + s) * NB + n]
+                if i == 0:
+                    got[s, pl.ds(row0, 16), :] = total
+                else:
+                    pick[i - 1, s] = total
+            if i > 0:
+                send(pick.at[i - 1], got.at[:, pl.ds(row0, 16), :], as_.at[4], ar.at[4], (to, y))
+
+    late = slab | (role == 3) | (role == 14)
+
+    @pl.when(jnp.logical_not(late))
+    def _():
+        deliver()
 
     wait_recv(gbuf.at[pl.ds(0, 7)], gr)
 
@@ -318,6 +337,10 @@
     lax.fori_loop(1, 8, body, 0)
     out_ref[...] = (acc[...] + product(7)).astype(jnp.bfloat16)
 
+    @pl.when(late)
+    def _():
+        deliver()
+
     wait_recv(got.at[:, pl.ds(0, 112), :], ar.at[4])
     owned_ref[0] = got[...]
 
@@ -329,16 +352,9 @@
     def _():
         wait_send(wbuf.at[pl.ds(0, 3), pl.ds(0, 512), :], zs)
 
-    @pl.when((role == 5) | (role == 12))
+    @pl.when(stop)
     def _():
         wait_send(wbuf.at[pl.ds(0, 2)], zs)
-
-    @pl.when(
-        (role == 3) | (role == 4) | (role == 6) | (role == 7)
-        | (role == 10) | (role == 11) | (role == 13) | (role == 14)
-    )
-    def _():
-        wait_send(wbuf.at[pl.ds(0, 1)], zs)
 
     wait_send(wbuf.at[pl.ds(0, 2)], xs)
     wait_send(wbuf.at[pl.ds(0, 1)], rs)
@@ -347,16 +363,31 @@
     wait_send(half, as_.at[0])
     wait_send(xsum.at[pl.ds(0, 3)], as_.at[1])
 
-    @pl.when(z < PIECES)
+    @pl.when(owner)
     def _():
         wait_send(zsum.at[pl.ds(0, PIECES - 1)], as_.at[2])
         wait_send(zrecv.at[pl.ds(0, NZ - 1)], as_.at[3])
 
-    @pl.when(z >= PIECES)
+    @pl.when(jnp.logical_not(owner))
     def _():
         wait_send(zsum, as_.at[2])
 
     wait_send(pick, as_.at[4])
+
+
+def write(a_ref, b_ref, out_ref, owned_ref, a, b, sems):
+    rows = [pl.ds(48 * i, 48) for i in range(4)]
+    first = [pltpu.make_async_copy(a_ref.at[r], a.at[r], sems.at[i]) for i, r in enumerate(rows)]
+    first += [pltpu.make_async_copy(b_ref, b, sems.at[4])]
+    last = [pltpu.make_async_copy(a.at[r], out_ref.at[r], sems.at[5 + i]) for i, r in enumerate(rows)]
+    last += [pltpu.make_async_copy(b, owned_ref, sems.at[9])]
+    for copy in first:
+        copy.start()
+    for one, two in zip(first, last):
+        one.wait()
+        two.start()
+    for two in last:
+        two.wait()
 
 
 def local(activations, out_grads, kv_weight, block_ids, block_owner):
@@ -380,7 +411,7 @@
             dma((NB + 1,)),
         ],
     )(block_ids, block_owner, activations, out_grads)
-    return pl.pallas_call(
+    result = pl.pallas_call(
         kernel,
         name="kv_backward",
         out_shape=(
@@ -398,10 +429,10 @@
             pltpu.VMEM((NB, 64, BLK), f32),
             pltpu.VMEM((NX, NB, 16, BLK), f32),
             pltpu.VMEM((NX, NB, 16, BLK), f32),
-            pltpu.VMEM((PIECES, 8, BLK), f32),
-            pltpu.VMEM((NZ, 8, BLK), f32),
-            pltpu.VMEM((8, BLK), f32),
-            pltpu.VMEM((PIECES, 8, BLK), f32),
+            pltpu.VMEM((PIECES, 16, BLK), f32),
+            pltpu.VMEM((NZ, 16, BLK), f32),
+            pltpu.VMEM((16, BLK), f32),
+            pltpu.VMEM((PIECES, 16, BLK), f32),
             pltpu.VMEM((7, CAP, 16, BLK), f32),
             pltpu.VMEM((CAP, BLK, BLK), f32),
             dma((4,)), dma, dma, dma, dma, dma, dma, dma((5,)),
@@ -409,6 +440,21 @@
         ],
         compiler_params=pltpu.CompilerParams(collective_id=0, has_side_effects=True),
     )(sel, part, out_grads, kv_weight)
+    return pl.pallas_call(
+        write,
+        name="write",
+        out_shape=(
+            jax.ShapeDtypeStruct((192, 1024), bf16),
+            jax.ShapeDtypeStruct((1, CAP, BLK, BLK), f32),
+        ),
+        in_specs=[any_space] * 2,
+        out_specs=(any_space, any_space),
+        scratch_shapes=[
+            pltpu.VMEM((192, 1024), bf16),
+            pltpu.VMEM((1, CAP, BLK, BLK), f32),
+            dma((10,)),
+        ],
+    )(*result)
 
 
 def solution(mesh):

time: 75.6 us -> 72.5 us (0.959)
  the two profiles are of different devices: /device:TPU:57 before, /device:TPU:90 now
where the time goes in v2:
time: 72.5 us; the launch traced here: 72.3 us
  Pallas kernels  71.6 us (99%)
    pallas_call x1, Pallas kernels, local(): pl.pallas_call(kernel, name='kv_backward', out_shape=(jax.ShapeDtypeStruc...  66.2 us
    pallas_call x1, Pallas kernels, local(): pl.pallas_call(block_terms, name='block_terms', out_shape=(jax.ShapeDtype...  3.6 us
    pallas_call x1, Pallas kernels, local(): pl.pallas_call(write, name='write', out_shape=(jax.ShapeDtypeStruct((192,...  1.84 us

profile of v2, /device:TPU:90, one launch (start us, length us, event | category | flops | bytes accessed | tf_op | source)
XLA Modules:
  0.0 72.3 jit_solution(9199272498312961075)
XLA Ops:
  0.6 3.6 %block_terms.1 = (f32[2,6,64,128]{3,2,1,0:T(8,128)}, f32[1,96]{1,0:T(1,128)}) custom-call(s32[1,6]{1,0:T(1,128)} %ids_ref.1, s32[1,6]{1,0:T(1,128)} %owner_ref.1, bf16[192,8192]{1,0:T(8,128)(2,1)} %x_hbm.1, bf16[192,256]{1,0:T(8,128)(2,1)} %g_hbm.3), custom_call_target="tpu_custom_call" | custom-call | tf_op jit(solution)/shard_map/block_terms/pallas_call | solution.py:399
  4.2 66.2 %kv_backward.1 = (bf16[192,1024]{1,0:T(8,128)(2,1)}, f32[1,2,128,128]{3,2,1,0:T(8,128)}) custom-call(f32[1,96]{1,0:T(1,128)} %get-tuple-element.6.sel_ref, f32[2,6,64,128]{3,2,1,0:T(8,128)} %get-tuple-element.7.part_hbm, bf16[192,256]{1,0:T(8,128)(2,1)} %g_hbm.3, bf16[64,256]{1,0:T(8,128)(2,1)} %w_hbm.1), custom_call_target="tpu_custom_call" | custom-call | tf_op jit(solution)/shard_map/kv_backward/pallas_call | solution.py:414
  70.4 1.8 %write.1 = (bf16[192,1024]{1,0:T(8,128)(2,1)}, f32[1,2,128,128]{3,2,1,0:T(8,128)}) custom-call(bf16[192,1024]{1,0:T(8,128)(2,1)} %get-tuple-element.8.a_ref, f32[1,2,128,128]{3,2,1,0:T(8,128)} %get-tuple-element.9.b_ref), custom_call_target="tpu_custom_call" | custom-call | tf_op jit(solution)/shard_map/write/pallas_call | solution.py:443

commit v3 on v2

--- a/solution.py
+++ b/solution.py
@@ -50,7 +50,7 @@
 def kernel(
     sel_ref, part_hbm, g_hbm, w_hbm, out_ref, owned_ref,
     wbuf, wown, gbuf, acc, part, half, xsum, xrecv, zsum, zrecv, mine, full, pick, got,
-    load_sem, shard_ss, zs, xs, rs, cs, gs, as_, zr, xr, xl, x2, cr, gr, ar,
+    load_sem, shard_ss, zs, xs, rs, cs, gs, as_, hs, zr, xr, xl, x2, cr, gr, ar,
 ):
     dp = lax.axis_index("dp")
     y = lax.axis_index("tensor")
@@ -106,7 +106,7 @@
 
     barrier = pltpu.get_barrier_semaphore()
     peers = [dev(x, (y + i) % NY, z, c) for i in range(1, NY)]
-    peers += [dev(x, y, (z + i) % NZ, c) for i in range(1, NZ)]
+    peers += [dev(x, y, (z + i) % NZ, c) for i in (1, NZ - 1)]
     peers += [dev((x + i) % NX, y, z, c) for i in range(1, NX)]
     peers += [dev((x + i) % NX, y, z, 1 - c) for i in range(NX)]
     for p in peers:
@@ -115,7 +115,38 @@
     load_g.wait()
     load_p.wait()
     load_w.wait()
-    pl.semaphore_wait(barrier, len(peers))
+
+    def tell(sem, dz):
+        pl.semaphore_signal(sem, inc=1, device_id=dev(x, y, (z + dz + NZ) % NZ, c), device_id_type=MESH)
+
+    parent = jnp.where((role == 2) | (role == 4) | (role == 6), 1, jnp.where(
+        (role == 5) | (role == 7), -2, jnp.where((role == 10) | (role == 12), 2, jnp.where(
+            (role == 8) | (role == 11) | (role == 13) | (role == 15), -1, 1))))
+
+    @pl.when(jnp.logical_not(slab | (role == 3) | (role == 14)))
+    def _():
+        tell(barrier, parent)
+
+    @pl.when(role == 3)
+    def _():
+        tell(barrier, -3)
+        tell(barrier, -2)
+
+    @pl.when(role == 14)
+    def _():
+        tell(barrier, 2)
+        tell(barrier, 3)
+
+    pl.semaphore_wait(barrier, len(peers) + jnp.where(slab | stop, 2, 0))
+
+    def told(n):
+        pl.semaphore_wait(hs.at[n], 2)
+        if n < 2:
+            tell(hs.at[n + 1], 2 << n)
+            tell(hs.at[n + 1], -(2 << n))
+
+    tell(hs.at[0], 1)
+    tell(hs.at[0], -1)
 
     yd = z // 2
     d = (y - yd + NY) % NY
@@ -168,6 +199,9 @@
         s = xrecv[0] + xrecv[1] + xrecv[2] + xrecv[3]
         zsum[...] = s
 
+    def out_step():
+        told(2)
+
         def body(i, carry):
             @pl.when(i != piece)
             def _():
@@ -202,17 +236,21 @@
     def _():
         local_w.wait()
         spread(0, hown)
+        told(0)
+        take(1, hown)
+        told(1)
 
         def body(j, carry):
             take(j, hown)
             return carry
 
-        lax.fori_loop(1, 8, body, 0)
+        lax.fori_loop(2, 8, body, 0)
         core_step()
         take(0, 1 - hown)
         take(1, 1 - hown)
         x_step()
         send_g()
+        out_step()
 
         def body2(j, carry):
             take(j, 1 - hown)
@@ -233,11 +271,15 @@
 
     @pl.when(first)
     def _():
-        units(0, 3)
+        told(0)
+        units(0, 1)
+        told(1)
+        units(1, 3)
         core_step()
         units(3, 5)
         x_step()
         send_g()
+        out_step()
         units(5, 8)
         z_step()
 
@@ -245,8 +287,11 @@
 
     @pl.when(jnp.logical_not(slab | first))
     def _():
+        told(0)
         core_step()
+        told(1)
         x_step()
+        out_step()
         send_g()
         units(0, 6)
 
@@ -435,7 +480,7 @@
             pltpu.VMEM((PIECES, 16, BLK), f32),
             pltpu.VMEM((7, CAP, 16, BLK), f32),
             pltpu.VMEM((CAP, BLK, BLK), f32),
-            dma((4,)), dma, dma, dma, dma, dma, dma, dma((5,)),
+            dma((4,)), dma, dma, dma, dma, dma, dma, dma((5,)), pltpu.SemaphoreType.REGULAR((3,)),
             dma((16,)), dma((8,)), dma((8,)), dma((8,)), dma((8,)), dma, dma((5,)),
         ],
         compiler_params=pltpu.CompilerParams(collective_id=0, has_side_effects=True),

time: 72.5 us -> 68.3 us (0.942)
  the two profiles are of different devices: /device:TPU:90 before, /device:TPU:1 now
where the time goes in v3:
time: 68.3 us; the launch traced here: 66.9 us
  Pallas kernels  66.3 us (97%)
    pallas_call x1, Pallas kernels, local(): pl.pallas_call(kernel, name='kv_backward', out_shape=(jax.ShapeDtypeStruc...  60.9 us
    pallas_call x1, Pallas kernels, local(): pl.pallas_call(block_terms, name='block_terms', out_shape=(jax.ShapeDtype...  3.6 us
    pallas_call x1, Pallas kernels, local(): pl.pallas_call(write, name='write', out_shape=(jax.ShapeDtypeStruct((192,...  1.84 us

profile of v3, /device:TPU:1, one launch (start us, length us, event | category | flops | bytes accessed | tf_op | source)
XLA Modules:
  0.0 66.9 jit_solution(12096800411592597493)
XLA Ops:
  0.6 3.6 %block_terms.1 = (f32[2,6,64,128]{3,2,1,0:T(8,128)}, f32[1,96]{1,0:T(1,128)}) custom-call(s32[1,6]{1,0:T(1,128)} %ids_ref.1, s32[1,6]{1,0:T(1,128)} %owner_ref.1, bf16[192,8192]{1,0:T(8,128)(2,1)} %x_hbm.1, bf16[192,256]{1,0:T(8,128)(2,1)} %g_hbm.3), custom_call_target="tpu_custom_call" | custom-call | tf_op jit(solution)/shard_map/block_terms/pallas_call | solution.py:444
  4.2 60.9 %kv_backward.1 = (bf16[192,1024]{1,0:T(8,128)(2,1)}, f32[1,2,128,128]{3,2,1,0:T(8,128)}) custom-call(f32[1,96]{1,0:T(1,128)} %get-tuple-element.6.sel_ref, f32[2,6,64,128]{3,2,1,0:T(8,128)} %get-tuple-element.7.part_hbm, bf16[192,256]{1,0:T(8,128)(2,1)} %g_hbm.3, bf16[64,256]{1,0:T(8,128)(2,1)} %w_hbm.1), custom_call_target="tpu_custom_call" | custom-call | tf_op jit(solution)/shard_map/kv_backward/pallas_call | solution.py:459
  65.1 1.8 %write.1 = (bf16[192,1024]{1,0:T(8,128)(2,1)}, f32[1,2,128,128]{3,2,1,0:T(8,128)}) custom-call(bf16[192,1024]{1,0:T(8,128)(2,1)} %get-tuple-element.8.a_ref, f32[1,2,128,128]{3,2,1,0:T(8,128)} %get-tuple-element.9.b_ref), custom_call_target="tpu_custom_call" | custom-call | tf_op jit(solution)/shard_map/write/pallas_call | solution.py:488

commit v4 on v3

--- a/solution.py
+++ b/solution.py
@@ -244,13 +244,15 @@
             take(j, hown)
             return carry
 
-        lax.fori_loop(2, 8, body, 0)
+        lax.fori_loop(2, 4, body, 0)
         core_step()
+        lax.fori_loop(4, 7, body, 0)
+        x_step()
+        out_step()
+        lax.fori_loop(7, 8, body, 0)
+        send_g()
         take(0, 1 - hown)
         take(1, 1 - hown)
-        x_step()
-        send_g()
-        out_step()
 
         def body2(j, carry):
             take(j, 1 - hown)

time: 68.3 us -> 67.4 us (0.987); the launches traced: 66.9 us -> 66.9 us
  no operation moved by 1% of the time
where the time goes in v4:
time: 67.4 us; the launch traced here: 66.9 us
  Pallas kernels  66.3 us (98%)
    pallas_call x1, Pallas kernels, local(): pl.pallas_call(kernel, name='kv_backward', out_shape=(jax.ShapeDtypeStruc...  60.9 us
    pallas_call x1, Pallas kernels, local(): pl.pallas_call(block_terms, name='block_terms', out_shape=(jax.ShapeDtype...  3.6 us
    pallas_call x1, Pallas kernels, local(): pl.pallas_call(write, name='write', out_shape=(jax.ShapeDtypeStruct((192,...  1.84 us

profile of v4, /device:TPU:1, one launch (start us, length us, event | category | flops | bytes accessed | tf_op | source)
XLA Modules:
  0.0 66.9 jit_solution(11706083563330671361)
XLA Ops:
  0.6 3.6 %block_terms.1 = (f32[2,6,64,128]{3,2,1,0:T(8,128)}, f32[1,96]{1,0:T(1,128)}) custom-call(s32[1,6]{1,0:T(1,128)} %ids_ref.1, s32[1,6]{1,0:T(1,128)} %owner_ref.1, bf16[192,8192]{1,0:T(8,128)(2,1)} %x_hbm.1, bf16[192,256]{1,0:T(8,128)(2,1)} %g_hbm.3), custom_call_target="tpu_custom_call" | custom-call | tf_op jit(solution)/shard_map/block_terms/pallas_call | solution.py:446
  4.2 60.9 %kv_backward.1 = (bf16[192,1024]{1,0:T(8,128)(2,1)}, f32[1,2,128,128]{3,2,1,0:T(8,128)}) custom-call(f32[1,96]{1,0:T(1,128)} %get-tuple-element.6.sel_ref, f32[2,6,64,128]{3,2,1,0:T(8,128)} %get-tuple-element.7.part_hbm, bf16[192,256]{1,0:T(8,128)(2,1)} %g_hbm.3, bf16[64,256]{1,0:T(8,128)(2,1)} %w_hbm.1), custom_call_target="tpu_custom_call" | custom-call | tf_op jit(solution)/shard_map/kv_backward/pallas_call | solution.py:461
  65.1 1.8 %write.1 = (bf16[192,1024]{1,0:T(8,128)(2,1)}, f32[1,2,128,128]{3,2,1,0:T(8,128)}) custom-call(bf16[192,1024]{1,0:T(8,128)(2,1)} %get-tuple-element.8.a_ref, f32[1,2,128,128]{3,2,1,0:T(8,128)} %get-tuple-element.9.b_ref), custom_call_target="tpu_custom_call" | custom-call | tf_op jit(solution)/shard_map/write/pallas_call | solution.py:490
